TPU v7x, 512 devices: a whole 4x4x16 slice. The times are simulated.
512 devices in a mesh: ctx: 128 (over x, z, core), head: 4 (over y).
Axes of the slice: x: 4, y: 4, z: 16, core: 2. Of those that a mesh axis runs over, the one named last changes fastest.
Arguments:
- query: bfloat16 [16384, 2048], P('ctx', 'head'), may hold values from -5 to 5, as said below
- key: bfloat16 [16384, 128], P('ctx'), may hold values from -5 to 5, as said below
- value: bfloat16 [16384, 128], P('ctx'), may hold values from -6 to 6
- grad_out: bfloat16 [16384, 2048], P('ctx', 'head'), may hold values from -6 to 6
- doc_lengths: int32 [32], replicated, may hold values from 1 to 1024, 16384 in all
Outputs:
- attention_out: bfloat16 [16384, 2048], P('ctx', 'head')
- grad_query: bfloat16 [16384, 2048], P('ctx', 'head')
- grad_key: bfloat16 [16384, 128], P('ctx')
- grad_value: bfloat16 [16384, 128], P('ctx')
Inputs may be any that keep to these rules, and one draw needn't show every extreme that they name: `doc_lengths`: positive lengths of the documents in sequence order, summing to 16384; the longest is exactly 1024. `query`: real values. `key`: real values.
All inputs are finite; a program needn't handle non-finite values.
Results may differ from a plain program's by a relative error of at most 0.014.
Values may be sent and summed in bfloat16 or wider, within the bound.
No kernel may reach another device: no remote copies, remote signals or barrier semaphores. Data moves between devices by JAX's collectives and lax.ppermute only.
A program may use at most 64 MiB of HBM per device.

v0:
```python
import jax
import jax.numpy as jnp
from jax import lax
from jax.experimental import pallas as pl
from jax.experimental.pallas import tpu as pltpu
from jax.sharding import PartitionSpec as P


HD = 128
STRETCH = 64
N_CTX = 128
N_HEAD = 4
LAST = 2 * N_CTX - 1
CHIP = 2
OFFSETS = (0, 4, 2, 6, 1, 5, 3, 7, 8)
GROUP = 3 * STRETCH
SIDE = 9 * STRETCH
COLS = 2 * N_HEAD * STRETCH
DOCS = 32
NEG = -1e30
SCALE = HD**-0.5
LOG2E = 1.4426950408889634
NT = (((1,), (1,)), ((), ()))
NN = (((1,), (0,)), ((), ()))
BOTH = ("ctx", "head")
PAIRS = [[i, i + 1] for i in range(0, N_CTX, 2)]


def home(stretch, copy):
    if stretch < N_CTX:
        return stretch * N_HEAD + copy
    return (LAST - stretch) * N_HEAD + N_HEAD - 1 - copy


def along(array, by):
    pairs = [
        (home(s, copy), home(s + by, copy))
        for s in range(LAST + 1)
        if 0 <= s + by <= LAST
        for copy in range(2)
    ]
    return lax.ppermute(array, BOTH, pairs)


def across(array):
    pairs = [
        (i * N_HEAD + h, i * N_HEAD + N_HEAD - 1 - h) for i in range(N_CTX) for h in range(N_HEAD)
    ]
    return lax.ppermute(array, BOTH, pairs)


def place_of():
    index = lax.axis_index("ctx")
    lower = lax.axis_index("head") < N_HEAD // 2
    core = index % 2
    first = jnp.where(lower, index - core, LAST - index + core)
    return core, lower, (first, jnp.where(lower, first + 1, first - 1))


def prepare(docs_ref, query_ref, grad_ref, far_ref, both_ref, begin_ref):
    _, lower, stretches = place_of()
    rows = pl.ds(pl.multiple_of(jnp.where(lower, 0, STRETCH), STRETCH), STRETCH)
    for h in range(N_HEAD):
        part = slice(h * HD, (h + 1) * HD)
        own = h * STRETCH
        far = (h + N_HEAD) * STRETCH
        both_ref[own : own + STRETCH, :] = query_ref[rows, part]
        both_ref[far : far + STRETCH, :] = far_ref[:STRETCH, part]
        own, far = own + COLS, far + COLS
        both_ref[own : own + STRETCH, :] = grad_ref[rows, part]
        both_ref[far : far + STRETCH, :] = far_ref[STRETCH:, part]
    inner = lax.broadcasted_iota(jnp.int32, (8, COLS), 1) % STRETCH
    for side in range(2):
        place = stretches[side] * STRETCH + inner
        begin = jnp.zeros((8, COLS), jnp.int32)
        end = jnp.int32(0)
        for k in range(DOCS):
            end = end + docs_ref[k]
            begin = jnp.where(place >= end, end, begin)
        begin_ref[:, side * COLS : (side + 1) * COLS] = begin


def score(window_ref, both_ref, begin_ref, e_ref, dp_ref, stats_ref, s_sc):
    core, _, stretches = place_of()
    mine = jnp.where(core == 0, stretches[0], stretches[1])
    inner = lax.broadcasted_iota(jnp.int32, (STRETCH, COLS), 0)
    row = lax.broadcasted_iota(jnp.int32, (1, COLS), 1) % STRETCH
    for side in range(2):
        columns = slice(side * COLS, (side + 1) * COLS)
        q = both_ref[2 * side * COLS : (2 * side + 1) * COLS, :]
        do = both_ref[(2 * side + 1) * COLS : (2 * side + 2) * COLS, :]
        place = stretches[side] * STRETCH + row
        begin = begin_ref[:1, columns]
        peak = jnp.full((1, COLS), NEG, jnp.float32)
        for k in range(3):
            at = k * GROUP
            raw = lax.dot_general(
                window_ref[at : at + GROUP, :HD], q, NT, preferred_element_type=jnp.float32
            )
            for j in range(3):
                base = (mine - CHIP * OFFSETS[3 * k + j]) * STRETCH
                live = inner >= begin - base
                if k == 0 and j == 0:
                    live = live & (inner <= place - base)
                block = jnp.where(live, raw[j * STRETCH : (j + 1) * STRETCH], NEG)
                s_sc[at + j * STRETCH : at + (j + 1) * STRETCH, columns] = block
                peak = jnp.maximum(peak, jnp.max(block, axis=0, keepdims=True))
        total = jnp.zeros((1, COLS), jnp.float32)
        delta = jnp.zeros((1, COLS), jnp.float32)
        for k in range(3):
            at = slice(k * GROUP, (k + 1) * GROUP)
            e = jnp.exp2((s_sc[at, columns] - peak) * (SCALE * LOG2E))
            dp = lax.dot_general(
                window_ref[at, HD:], do, NT, preferred_element_type=jnp.float32
            )
            total = total + jnp.sum(e, axis=0, keepdims=True)
            delta = delta + jnp.sum(e * dp, axis=0, keepdims=True)
            e_ref[at, columns] = e.astype(jnp.bfloat16)
            dp_ref[at, columns] = dp
        rest = jnp.zeros((5, COLS), jnp.float32)
        stats_ref[:, columns] = jnp.concatenate([peak, total, delta, rest], axis=0)


def grads(window_ref, both_ref, e_ref, dp_ref, stats_ref, grad_ref, en_ref, ds_ref):
    core = lax.axis_index("ctx") % 2
    for k in range(3):
        at = slice(k * GROUP, (k + 1) * GROUP)
        dk = jnp.zeros((GROUP, HD), jnp.float32)
        dv = jnp.zeros((GROUP, HD), jnp.float32)
        for side in range(2):
            columns = slice(side * COLS, (side + 1) * COLS)
            q = both_ref[2 * side * COLS : (2 * side + 1) * COLS, :]
            do = both_ref[(2 * side + 1) * COLS : (2 * side + 2) * COLS, :]
            peaks = stats_ref[0:1, columns], stats_ref[8:9, columns]
            peak = jnp.maximum(*peaks)
            scales = [jnp.exp2((p - peak) * (SCALE * LOG2E)) for p in peaks]
            total = scales[0] * stats_ref[1:2, columns] + scales[1] * stats_ref[9:10, columns]
            delta = scales[0] * stats_ref[2:3, columns] + scales[1] * stats_ref[10:11, columns]
            delta = delta / total
            share = jnp.where(core == 0, scales[0], scales[1]) / total
            e = e_ref[at, columns].astype(jnp.float32) * share
            en = e.astype(jnp.bfloat16)
            ds = (e * (dp_ref[at, columns] - delta)).astype(jnp.bfloat16)
            dk = dk + lax.dot_general(ds, q, NN, preferred_element_type=jnp.float32)
            dv = dv + lax.dot_general(en, do, NN, preferred_element_type=jnp.float32)
            en_ref[at, columns] = en
            ds_ref[at, columns] = ds
        grad_ref[at, :HD] = (dk * SCALE).astype(jnp.bfloat16)
        grad_ref[at, HD:] = dv.astype(jnp.bfloat16)


def partial(window_ref, en_ref, ds_ref, keep_ref, send_ref):
    core = lax.axis_index("ctx") % 2
    out = lax.dot_general(
        window_ref[:, HD:].T, en_ref[...], NN, preferred_element_type=jnp.float32
    )
    dq = SCALE * lax.dot_general(
        window_ref[:, :HD].T, ds_ref[...], NN, preferred_element_type=jnp.float32
    )
    for at, both in ((0, out), (HD, dq)):
        one, two = both[:, :COLS], both[:, COLS:]
        keep_ref[at : at + HD, :] = jnp.where(core == 0, one, two)
        send_ref[at : at + HD, :] = jnp.where(core == 0, two, one).astype(jnp.bfloat16)


def finish(sent_ref, keep_ref, out_ref, dq_ref, far_out_ref):
    core = lax.axis_index("ctx") % 2
    came = sent_ref[pl.ds(pl.multiple_of((1 - core) * 2 * HD, 2 * HD), 2 * HD), :]
    both = (keep_ref[...] + came.astype(jnp.float32)).astype(jnp.bfloat16)
    out = both[:HD].T
    dq = both[HD:].T
    for h in range(N_HEAD):
        part = slice(h * HD, (h + 1) * HD)
        own = slice(h * STRETCH, (h + 1) * STRETCH)
        far = slice((h + N_HEAD) * STRETCH, (h + N_HEAD + 1) * STRETCH)
        out_ref[:, part] = out[own]
        dq_ref[:, part] = dq[own]
        far_out_ref[:STRETCH, part] = out[far]
        far_out_ref[STRETCH:, part] = dq[far]


VMEM = pl.BlockSpec(memory_space=pltpu.VMEM)
SMEM = pl.BlockSpec(memory_space=pltpu.SMEM)
F32 = jnp.float32


def shaped(rows, columns, dtype=jnp.bfloat16):
    return jax.ShapeDtypeStruct((rows, columns), dtype)


def run(kernel, outs, args, flops, scratch=(), scalars=0):
    return pl.pallas_call(
        kernel,
        out_shape=outs,
        in_specs=[SMEM] * scalars + [VMEM] * (len(args) - scalars),
        out_specs=(VMEM,) * len(outs),
        scratch_shapes=scratch,
        compiler_params=pltpu.CompilerParams(vmem_limit_bytes=20 << 20),
        cost_estimate=pl.CostEstimate(flops=flops, bytes_accessed=8 * COLS * HD, transcendentals=0),
    )(*args)


def prepared(docs, query, grad, far):
    outs = (shaped(2 * COLS, HD), shaped(8, 2 * COLS, jnp.int32))
    return run(prepare, outs, (docs, query, grad, far), DOCS * COLS, scalars=1)


def scored(window, both, begin):
    outs = (shaped(SIDE, 2 * COLS), shaped(SIDE, 2 * COLS, F32), shaped(8, 2 * COLS, F32))
    work = 8 * SIDE * COLS * HD
    return run(score, outs, (window, both, begin), work, (pltpu.VMEM((SIDE, 2 * COLS), F32),))


def graded(window, both, e, dp, stats):
    outs = (shaped(SIDE, 2 * HD), shaped(SIDE, 2 * COLS), shaped(SIDE, 2 * COLS))
    return run(grads, outs, (window, both, e, dp, stats), 8 * SIDE * COLS * HD)


def parted(window, en, ds):
    outs = (shaped(2 * HD, COLS, F32), shaped(2 * HD, COLS))
    return run(partial, outs, (window, en, ds), 8 * SIDE * COLS * HD)


def finished(sent, keep):
    half, both = shaped(STRETCH, N_HEAD * HD), shaped(2 * STRETCH, N_HEAD * HD)
    return run(finish, (half, half, both), (sent, keep), COLS * HD)


def paired(array):
    return lax.all_gather(array, "ctx", axis_index_groups=PAIRS, axis=0, tiled=True)


def body(query, key, value, grad_out, doc_lengths):
    lower = lax.axis_index("head") < N_HEAD // 2
    mine = jnp.where(lower, 0, STRETCH)
    other = STRETCH - mine

    def pick(array, first):
        return lax.dynamic_slice_in_dim(array, first, STRETCH, 0)

    far = across(jnp.concatenate([pick(query, other), pick(grad_out, other)], axis=0))
    own = jnp.concatenate([pick(key, mine), pick(value, mine)], axis=1)
    at_4 = along(own, 4 * CHIP)
    two = jnp.concatenate([own, at_4], axis=0)
    at_2_6 = along(two, 2 * CHIP)
    at_8 = along(at_4, 4 * CHIP)
    four = jnp.concatenate([two, at_2_6], axis=0)
    odd = along(four, CHIP)
    parity = jnp.concatenate([four, odd, at_8], axis=0)
    own_rows, begin = prepared(doc_lengths, query, grad_out, far)
    both = paired(own_rows)
    e, dp, stats = scored(parity, both, begin)
    stats = paired(stats)
    grad, en, ds = graded(parity, both, e, dp, stats)
    keep, send = parted(parity, en, ds)
    out, dq, far_out = finished(paired(send), keep)

    def block(start, stop):
        return grad[start * STRETCH : stop * STRETCH]

    def home_by(array, chips):
        return along(array.astype(jnp.bfloat16), -chips * CHIP).astype(jnp.float32)

    eighth = home_by(block(8, 9), 4)
    even = block(0, 4).astype(F32) + home_by(block(4, 8), 1)
    first = even[: 2 * STRETCH] + home_by(even[2 * STRETCH :], 2)
    back = across(far_out)
    total = (first[:STRETCH] + home_by(first[STRETCH:] + eighth, 4)).astype(jnp.bfloat16)
    copies = jnp.broadcast_to(total, (N_HEAD,) + total.shape)
    shared = lax.all_to_all(copies, "head", 0, 0)
    shared = shared.astype(jnp.float32)
    kv = jnp.concatenate([shared[0] + shared[1], shared[2] + shared[3]], axis=0)
    kv = kv.astype(jnp.bfloat16)

    def placed(here, there):
        return jnp.where(
            lower, jnp.concatenate([here, there]), jnp.concatenate([there, here])
        )

    return (
        placed(out, back[:STRETCH]),
        placed(dq, back[STRETCH:]),
        kv[:, :HD],
        kv[:, HD:],
    )


def solution(mesh):
    in_specs = (P("ctx", "head"), P("ctx", None), P("ctx", None), P("ctx", "head"), P())
    out_specs = (P("ctx", "head"), P("ctx", "head"), P("ctx", None), P("ctx", None))

    return jax.shard_map(body, mesh=mesh, in_specs=in_specs, out_specs=out_specs, check_vma=False)
```

profile of v0, /device:TPU:6, one launch (start us, length us, event | category | flops | bytes accessed | tf_op | source)
XLA Modules:
  0.0 83.5 jit_solution(9500757138817688601)
XLA Ops:
  0.7 0.7 copy-done
  1.4 0.7 constant_dynamic-slice_fusion.2
  2.1 9.1 %collective-permute-start = (bf16[64,256]{1,0:T(8,128)(2,1)S(1)}, bf16[64,256]{1,0:T(8,128)(2,1)S(1)}, u32[]{:S(2)}, u32[]{:S(2)}) collective-permute-start(bf16[64,256]{1,0:T(8,128)(2,1)S(1)} %get-tuple-element.36), channel_id=1, source_target_pairs={{0,32},{1,33},{4,36},{5,37},{8,40},{9,41},{12,44},{13,45},{16,48},... | collective-permute-start | bytes 98312 | tf_op jit(solution)/shard_map/ppermute | solution.py:42
  11.2 0.8 %constant_dynamic-slice_fusion.1 = bf16[64,512]{1,0:T(8,128)(2,1)S(1)} fusion(bf16[128,512]{1,0:T(8,128)(2,1)} %query_ref.1, s32[]{:T(128)S(6)} %select_n.24), kind=kLoop, calls=%fused_computation.29 | loop fusion | bytes 131076 | tf_op jit(solution)/shard_map/dynamic_slice | solution.py:239
  12.1 0.8 %constant_dynamic-slice_fusion = bf16[64,512]{1,0:T(8,128)(2,1)S(1)} fusion(bf16[128,512]{1,0:T(8,128)(2,1)} %grad_ref.1, s32[]{:T(128)S(6)} %select_n.24), kind=kLoop, calls=%fused_computation.28 | loop fusion | bytes 131076 | tf_op jit(solution)/shard_map/dynamic_slice | solution.py:239
  12.9 8.8 %collective-permute-start.4 = (bf16[128,512]{1,0:T(8,128)(2,1)S(1)}, bf16[128,512]{1,0:T(8,128)(2,1)S(1)}, u32[]{:S(2)}, u32[]{:S(2)}) collective-permute-start(bf16[128,512]{1,0:T(8,128)(2,1)S(1)} %pad_maximum_fusion.1), channel_id=1, source_target_pairs={{0,3},{1,2},{2,1},{3,0},{4,7},{5,6},{6,5},{7,4},{8,11},{9,10},{10,... | collective-permute-start | bytes 393224 | tf_op jit(solution)/shard_map/ppermute | solution.py:49
  21.8 3.4 %collective-permute-start.1 = (bf16[128,256]{1,0:T(8,128)(2,1)S(1)}, bf16[128,256]{1,0:T(8,128)(2,1)S(1)}, u32[]{:S(2)}, u32[]{:S(2)}) collective-permute-start(bf16[128,256]{1,0:T(8,128)(2,1)S(1)} %pad_maximum_fusion.2), channel_id=1, source_target_pairs={{0,16},{1,17},{4,20},{5,21},{8,24},{9,25},{12,28},{13,29},{16,32},... | collective-permute-start | bytes 196616 | tf_op jit(solution)/shard_map/ppermute | solution.py:42
  25.2 2.2 %collective-permute-start.3 = (bf16[64,256]{1,0:T(8,128)(2,1)S(1)}, bf16[64,256]{1,0:T(8,128)(2,1)S(1)}, u32[]{:S(2)}, u32[]{:S(2)}) collective-permute-start(bf16[64,256]{1,0:T(8,128)(2,1)S(1)} %collective-permute-done), channel_id=1, source_target_pairs={{0,32},{1,33},{4,36},{5,37},{8,40},{9,41},{12,44},{13,45},{16,48},... | collective-permute-start | bytes 98312 | tf_op jit(solution)/shard_map/ppermute | solution.py:42
  27.4 3.8 %collective-permute-done.1 = bf16[128,256]{1,0:T(8,128)(2,1)S(1)} collective-permute-done((bf16[128,256]{1,0:T(8,128)(2,1)S(1)}, bf16[128,256]{1,0:T(8,128)(2,1)S(1)}, u32[]{:S(2)}, u32[]{:S(2)}) %collective-permute-start.1) | collective-permute-done | bytes 65568 | tf_op jit(solution)/shard_map/ppermute | solution.py:42
  31.2 3.4 %collective-permute-start.2 = (bf16[256,256]{1,0:T(8,128)(2,1)S(1)}, bf16[256,256]{1,0:T(8,128)(2,1)S(1)}, u32[]{:S(2)}, u32[]{:S(2)}) collective-permute-start(bf16[256,256]{1,0:T(8,128)(2,1)S(1)} %pad_maximum_fusion), channel_id=1, source_target_pairs={{0,8},{1,9},{4,12},{5,13},{8,16},{9,17},{12,20},{13,21},{16,24},{1... | collective-permute-start | bytes 393224 | tf_op jit(solution)/shard_map/ppermute | solution.py:42
  34.7 0.7 shard_map.84
  35.4 2.2 %all_gather.9.both_ref = bf16[2048,128]{1,0:T(8,128)(2,1)S(1)} all-gather(bf16[1024,128]{1,0:T(8,128)(2,1)S(1)} %get-tuple-element.17), channel_id=1, replica_groups={{0,4},{8,12},{16,20},{24,28},{32,36},{40,44},{48,52},{56,60},{64,68},{7..., dimensions={0}, use_global_device_ids=true | all-gather | bytes 786432 | tf_op jit(solution)/shard_map/all_gather | solution.py:230
  37.5 2.7 %collective-permute-done.2 = bf16[256,256]{1,0:T(8,128)(2,1)S(1)} collective-permute-done((bf16[256,256]{1,0:T(8,128)(2,1)S(1)}, bf16[256,256]{1,0:T(8,128)(2,1)S(1)}, u32[]{:S(2)}, u32[]{:S(2)}) %collective-permute-start.2) | collective-permute-done | bytes 131104 | tf_op jit(solution)/shard_map/ppermute | solution.py:42
  40.2 1.3 %shard_map.85 = (bf16[576,1024]{1,0:T(8,128)(2,1)S(1)}, f32[576,1024]{1,0:T(8,128)S(1)}, f32[8,1024]{1,0:T(8,128)S(1)}) custom-call(bf16[576,256]{1,0:T(8,128)(2,1)S(1)} %constant_dynamic-update-slice_fusion.window_ref, bf16[2048,128]{1,0:T(8,128)(2,1)S(1)} %all_gather.9.both_ref, s32[8,1024]{1,0:T(8,128)S(1)} %get-tuple-element.18.begin_ref), custom_call_target="tpu_custom_call" | custom-call | flops 301989888 | bytes 524288 | tf_op jit(solution)/shard_map/pallas_call | solution.py:192
  41.5 1.9 %all_gather.10.stats_ref = f32[16,1024]{1,0:T(8,128)S(1)} all-gather(f32[8,1024]{1,0:T(8,128)S(1)} %get-tuple-element.21), channel_id=1, replica_groups={{0,4},{8,12},{16,20},{24,28},{32,36},{40,44},{48,52},{56,60},{64,68},{7..., dimensions={0}, use_global_device_ids=true | all-gather | bytes 98304 | tf_op jit(solution)/shard_map/all_gather | solution.py:230
  43.4 1.0 %shard_map.86 = (bf16[576,256]{1,0:T(8,128)(2,1)S(1)}, bf16[576,1024]{1,0:T(8,128)(2,1)S(1)}, bf16[576,1024]{1,0:T(8,128)(2,1)S(1)}) custom-call(bf16[576,256]{1,0:T(8,128)(2,1)S(1)} %constant_dynamic-update-slice_fusion.window_ref, bf16[2048,128]{1,0:T(8,128)(2,1)S(1)} %all_gather.9.both_ref, bf16[576,1024]{1,0:T(8,128)(2,1)S(1)} %get-tuple-element.19.e_ref, ...), custom_call_target="tpu_custom_call" | custom-call | flops 301989888 | bytes 524288 | tf_op jit(solution)/shard_map/pallas_call | solution.py:192
  44.3 1.9 %collective-permute-start.6 = (bf16[256,256]{1,0:T(8,128)(2,1)S(1)}, bf16[256,256]{1,0:T(8,128)(2,1)S(1)}, u32[]{:S(2)}, u32[]{:S(2)}) collective-permute-start(bf16[256,256]{1,0:T(8,128)(2,1)S(1)} %slice.49), channel_id=1, source_target_pairs={{8,0},{9,1},{12,4},{13,5},{16,8},{17,9},{20,12},{21,13},{24,16},{2... | collective-permute-start | bytes 393224 | tf_op jit(solution)/shard_map/ppermute | solution.py:42
  46.3 4.7 %collective-permute-start.8 = (bf16[64,256]{1,0:T(8,128)(2,1)S(1)}, bf16[64,256]{1,0:T(8,128)(2,1)S(1)}, u32[]{:S(2)}, u32[]{:S(2)}) collective-permute-start(bf16[64,256]{1,0:T(8,128)(2,1)S(1)} %slice.54), channel_id=1, source_target_pairs={{32,0},{33,1},{36,4},{37,5},{40,8},{41,9},{44,12},{45,13},{48,16},... | collective-permute-start | bytes 98312 | tf_op jit(solution)/shard_map/ppermute | solution.py:42
  51.0 0.6 shard_map.87
  51.7 0.1 collective-permute-done.6
  51.9 2.6 %collective-permute-start.7 = (bf16[128,256]{1,0:T(8,128)(2,1)S(1)}, bf16[128,256]{1,0:T(8,128)(2,1)S(1)}, u32[]{:S(2)}, u32[]{:S(2)}) collective-permute-start(bf16[128,256]{1,0:T(8,128)(2,1)S(1)} %slice.104), channel_id=1, source_target_pairs={{16,0},{17,1},{20,4},{21,5},{24,8},{25,9},{28,12},{29,13},{32,16},... | collective-permute-start | bytes 196616 | tf_op jit(solution)/shard_map/ppermute | solution.py:42
  54.4 2.2 %all_gather.11.sent_ref = bf16[512,512]{1,0:T(8,128)(2,1)S(1)} all-gather(bf16[256,512]{1,0:T(8,128)(2,1)S(1)} %get-tuple-element.24), channel_id=1, replica_groups={{0,4},{8,12},{16,20},{24,28},{32,36},{40,44},{48,52},{56,60},{64,68},{7..., dimensions={0}, use_global_device_ids=true | all-gather | bytes 786432 | tf_op jit(solution)/shard_map/all_gather | solution.py:230
  56.6 0.1 shard_map.88
  56.7 3.1 %collective-permute-start.5 = (bf16[128,512]{1,0:T(8,128)(2,1)S(1)}, bf16[128,512]{1,0:T(8,128)(2,1)S(1)}, u32[]{:S(2)}, u32[]{:S(2)}) collective-permute-start(bf16[128,512]{1,0:T(8,128)(2,1)S(1)} %get-tuple-element.27), channel_id=1, source_target_pairs={{0,3},{1,2},{2,1},{3,0},{4,7},{5,6},{6,5},{7,4},{8,11},{9,10},{10,... | collective-permute-start | bytes 393224 | tf_op jit(solution)/shard_map/ppermute | solution.py:49
  59.8 0.2 collective-permute-done.7
  60.1 6.8 %collective-permute-start.9 = (bf16[64,256]{1,0:T(8,128)(2,1)S(1)}, bf16[64,256]{1,0:T(8,128)(2,1)S(1)}, u32[]{:S(2)}, u32[]{:S(2)}) collective-permute-start(bf16[64,256]{1,0:T(8,128)(2,1)S(1)} %fusion.2), channel_id=1, source_target_pairs={{32,0},{33,1},{36,4},{37,5},{40,8},{41,9},{44,12},{45,13},{48,16},... | collective-permute-start | bytes 98312 | tf_op jit(solution)/shard_map/ppermute | solution.py:42
  66.9 2.9 %collective-permute-done.9 = bf16[64,256]{1,0:T(8,128)(2,1)S(1)} collective-permute-done((bf16[64,256]{1,0:T(8,128)(2,1)S(1)}, bf16[64,256]{1,0:T(8,128)(2,1)S(1)}, u32[]{:S(2)}, u32[]{:S(2)}) %collective-permute-start.9) | collective-permute-done | bytes 32800 | tf_op jit(solution)/shard_map/ppermute | solution.py:42
  69.8 0.6 broadcast_in_dim.3
  70.5 6.3 %all-to-all-start = ((bf16[4,64,256]{2,1,0:T(8,128)(2,1)}), bf16[4,64,256]{2,1,0:T(8,128)(2,1)S(1)}, u32[]{:S(2)}, u32[]{:S(2)}) async-start(bf16[4,64,256]{2,1,0:T(8,128)(2,1)} %broadcast_in_dim.3), calls=%async_computation | async-start | bytes 262144 | tf_op jit(solution)/shard_map/all_to_all | solution.py:270
  76.8 0.8 maximum_select_fusion
  77.6 5.2 %all-to-all-done = bf16[4,64,256]{2,1,0:T(8,128)(2,1)S(1)} async-done(((bf16[4,64,256]{2,1,0:T(8,128)(2,1)}), bf16[4,64,256]{2,1,0:T(8,128)(2,1)S(1)}, u32[]{:S(2)}, u32[]{:S(2)}) %all-to-all-start) | async-done | bytes 131104 | tf_op jit(solution)/shard_map/all_to_all | solution.py:270
  82.8 0.6 pad_maximum_fusion.3
  (31 shorter events, 0.2 us)
Async XLA Ops:
  0.6 0.8 copy-start
  0.6 34.0 %copy-start.1 = (bf16[128,512]{1,0:T(8,128)(2,1)S(1)}, bf16[128,512]{1,0:T(8,128)(2,1)}, u32[]{:S(2)}) copy-start(bf16[128,512]{1,0:T(8,128)(2,1)} %query_ref.1) | copy-start | bytes 393220
  0.7 34.0 %copy-start.2 = (bf16[128,512]{1,0:T(8,128)(2,1)S(1)}, bf16[128,512]{1,0:T(8,128)(2,1)}, u32[]{:S(2)}) copy-start(bf16[128,512]{1,0:T(8,128)(2,1)} %grad_ref.1) | copy-start | bytes 393220
  0.7 34.0 %copy-start.3 = (s32[32]{0:T(128)S(1)}, s32[32]{0:T(128)}, u32[]{:S(2)}) copy-start(s32[32]{0:T(128)} %docs_ref.1) | copy-start | bytes 388
  2.1 19.6 %collective-permute-start = (bf16[64,256]{1,0:T(8,128)(2,1)S(1)}, bf16[64,256]{1,0:T(8,128)(2,1)S(1)}, u32[]{:S(2)}, u32[]{:S(2)}) collective-permute-start(bf16[64,256]{1,0:T(8,128)(2,1)S(1)} %get-tuple-element.36), channel_id=1, source_target_pairs={{0,32},{1,33},{4,36},{5,37},{8,40},{9,41},{12,44},{13,45},{16,48},... | collective-permute-start | bytes 98312 | tf_op jit(solution)/shard_map/ppermute | solution.py:42
  12.9 21.7 %collective-permute-start.4 = (bf16[128,512]{1,0:T(8,128)(2,1)S(1)}, bf16[128,512]{1,0:T(8,128)(2,1)S(1)}, u32[]{:S(2)}, u32[]{:S(2)}) collective-permute-start(bf16[128,512]{1,0:T(8,128)(2,1)S(1)} %pad_maximum_fusion.1), channel_id=1, source_target_pairs={{0,3},{1,2},{2,1},{3,0},{4,7},{5,6},{6,5},{7,4},{8,11},{9,10},{10,... | collective-permute-start | bytes 393224 | tf_op jit(solution)/shard_map/ppermute | solution.py:49
  21.8 9.4 %collective-permute-start.1 = (bf16[128,256]{1,0:T(8,128)(2,1)S(1)}, bf16[128,256]{1,0:T(8,128)(2,1)S(1)}, u32[]{:S(2)}, u32[]{:S(2)}) collective-permute-start(bf16[128,256]{1,0:T(8,128)(2,1)S(1)} %pad_maximum_fusion.2), channel_id=1, source_target_pairs={{0,16},{1,17},{4,20},{5,21},{8,24},{9,25},{12,28},{13,29},{16,32},... | collective-permute-start | bytes 196616 | tf_op jit(solution)/shard_map/ppermute | solution.py:42
  25.2 15.0 %collective-permute-start.3 = (bf16[64,256]{1,0:T(8,128)(2,1)S(1)}, bf16[64,256]{1,0:T(8,128)(2,1)S(1)}, u32[]{:S(2)}, u32[]{:S(2)}) collective-permute-start(bf16[64,256]{1,0:T(8,128)(2,1)S(1)} %collective-permute-done), channel_id=1, source_target_pairs={{0,32},{1,33},{4,36},{5,37},{8,40},{9,41},{12,44},{13,45},{16,48},... | collective-permute-start | bytes 98312 | tf_op jit(solution)/shard_map/ppermute | solution.py:42
  31.2 9.0 %collective-permute-start.2 = (bf16[256,256]{1,0:T(8,128)(2,1)S(1)}, bf16[256,256]{1,0:T(8,128)(2,1)S(1)}, u32[]{:S(2)}, u32[]{:S(2)}) collective-permute-start(bf16[256,256]{1,0:T(8,128)(2,1)S(1)} %pad_maximum_fusion), channel_id=1, source_target_pairs={{0,8},{1,9},{4,12},{5,13},{8,16},{9,17},{12,20},{13,21},{16,24},{1... | collective-permute-start | bytes 393224 | tf_op jit(solution)/shard_map/ppermute | solution.py:42
  44.3 7.5 %collective-permute-start.6 = (bf16[256,256]{1,0:T(8,128)(2,1)S(1)}, bf16[256,256]{1,0:T(8,128)(2,1)S(1)}, u32[]{:S(2)}, u32[]{:S(2)}) collective-permute-start(bf16[256,256]{1,0:T(8,128)(2,1)S(1)} %slice.49), channel_id=1, source_target_pairs={{8,0},{9,1},{12,4},{13,5},{16,8},{17,9},{20,12},{21,13},{24,16},{2... | collective-permute-start | bytes 393224 | tf_op jit(solution)/shard_map/ppermute | solution.py:42
  46.3 13.8 %collective-permute-start.8 = (bf16[64,256]{1,0:T(8,128)(2,1)S(1)}, bf16[64,256]{1,0:T(8,128)(2,1)S(1)}, u32[]{:S(2)}, u32[]{:S(2)}) collective-permute-start(bf16[64,256]{1,0:T(8,128)(2,1)S(1)} %slice.54), channel_id=1, source_target_pairs={{32,0},{33,1},{36,4},{37,5},{40,8},{41,9},{44,12},{45,13},{48,16},... | collective-permute-start | bytes 98312 | tf_op jit(solution)/shard_map/ppermute | solution.py:42
  51.9 8.2 %collective-permute-start.7 = (bf16[128,256]{1,0:T(8,128)(2,1)S(1)}, bf16[128,256]{1,0:T(8,128)(2,1)S(1)}, u32[]{:S(2)}, u32[]{:S(2)}) collective-permute-start(bf16[128,256]{1,0:T(8,128)(2,1)S(1)} %slice.104), channel_id=1, source_target_pairs={{16,0},{17,1},{20,4},{21,5},{24,8},{25,9},{28,12},{29,13},{32,16},... | collective-permute-start | bytes 196616 | tf_op jit(solution)/shard_map/ppermute | solution.py:42
  56.7 10.1 %collective-permute-start.5 = (bf16[128,512]{1,0:T(8,128)(2,1)S(1)}, bf16[128,512]{1,0:T(8,128)(2,1)S(1)}, u32[]{:S(2)}, u32[]{:S(2)}) collective-permute-start(bf16[128,512]{1,0:T(8,128)(2,1)S(1)} %get-tuple-element.27), channel_id=1, source_target_pairs={{0,3},{1,2},{2,1},{3,0},{4,7},{5,6},{6,5},{7,4},{8,11},{9,10},{10,... | collective-permute-start | bytes 393224 | tf_op jit(solution)/shard_map/ppermute | solution.py:49
  60.1 9.7 %collective-permute-start.9 = (bf16[64,256]{1,0:T(8,128)(2,1)S(1)}, bf16[64,256]{1,0:T(8,128)(2,1)S(1)}, u32[]{:S(2)}, u32[]{:S(2)}) collective-permute-start(bf16[64,256]{1,0:T(8,128)(2,1)S(1)} %fusion.2), channel_id=1, source_target_pairs={{32,0},{33,1},{36,4},{37,5},{40,8},{41,9},{44,12},{45,13},{48,16},... | collective-permute-start | bytes 98312 | tf_op jit(solution)/shard_map/ppermute | solution.py:42
  70.5 12.3 %all-to-all-start = ((bf16[4,64,256]{2,1,0:T(8,128)(2,1)}), bf16[4,64,256]{2,1,0:T(8,128)(2,1)S(1)}, u32[]{:S(2)}, u32[]{:S(2)}) async-start(bf16[4,64,256]{2,1,0:T(8,128)(2,1)} %broadcast_in_dim.3), calls=%async_computation | async-start | bytes 262144 | tf_op jit(solution)/shard_map/all_to_all | solution.py:270
where the time goes:
time: 84.1 us; the launch traced here: 83.5 us
  starting transfers between devices  52.3 us (62%)
  waiting for transfers between devices  15 us (18%)
  blocking collectives  6.22 us (7%)
  local copies, waits for them, and re-layouts  3.85 us (5%)
  Pallas kernels  3.63 us (4%)
  other arithmetic  1.53 us (2%)
  between operations  0.96 us (1%)
    ppermute x8, starting transfers between devices, along(): return lax.ppermute(array, BOTH, pairs)  34.1 us
    ppermute x2, starting transfers between devices, across(): return lax.ppermute(array, BOTH, pairs)  11.9 us
    ppermute x8, waiting for transfers between devices, along(): return lax.ppermute(array, BOTH, pairs)  9.73 us
    all_to_all x1, starting transfers between devices, body(): shared = lax.all_to_all(copies, 'head', 0, 0)  6.32 us
    all_gather x3, blocking collectives, paired(): lax.all_gather(array, 'ctx', axis_index_groups=PAIRS, axis=0, tiled=True)  6.22 us
    all_to_all x1, waiting for transfers between devices, body(): shared = lax.all_to_all(copies, 'head', 0, 0)  5.22 us
    pallas_call x5, Pallas kernels, run(): pl.pallas_call(kernel, out_shape=outs, in_specs=[SMEM] * scalars + [VMEM]...  3.63 us
    dynamic_slice x4, local copies, waits for them, and re-layouts, pick(): return lax.dynamic_slice_in_dim(array, first, STRETCH, 0)  2.41 us
  transfers between devices with their start and end apart: 11, of which 6 were waited for; matrix products, arithmetic and copies ran while one was open for 3% of the time, Pallas kernels for 2%

commit v1 on v0

--- a/solution.py
+++ b/solution.py
@@ -57,18 +57,40 @@
     return core, lower, (first, jnp.where(lower, first + 1, first - 1))
 
 
+def settle(
+    out_ref, dq_ref, back_ref, kv_ref, all_out_ref, all_dq_ref, gk_ref, gv_ref, sems
+):
+    _, lower, _ = place_of()
+    here = pl.multiple_of(jnp.where(lower, 0, STRETCH), STRETCH)
+    there = pl.multiple_of(jnp.where(lower, STRETCH, 0), STRETCH)
+    moves = (
+        (out_ref, all_out_ref.at[pl.ds(here, STRETCH), :]),
+        (back_ref.at[:STRETCH, :], all_out_ref.at[pl.ds(there, STRETCH), :]),
+        (dq_ref, all_dq_ref.at[pl.ds(here, STRETCH), :]),
+        (back_ref.at[STRETCH:, :], all_dq_ref.at[pl.ds(there, STRETCH), :]),
+        (kv_ref.at[:, :HD], gk_ref),
+        (kv_ref.at[:, HD:], gv_ref),
+    )
+    copies = [pltpu.make_async_copy(a, b, sems.at[i]) for i, (a, b) in enumerate(moves)]
+    for copy in copies:
+        copy.start()
+    for copy in copies:
+        copy.wait()
+
+
 def prepare(docs_ref, query_ref, grad_ref, far_ref, both_ref, begin_ref):
     _, lower, stretches = place_of()
     rows = pl.ds(pl.multiple_of(jnp.where(lower, 0, STRETCH), STRETCH), STRETCH)
     for h in range(N_HEAD):
         part = slice(h * HD, (h + 1) * HD)
+        beyond = slice((h + N_HEAD) * HD, (h + N_HEAD + 1) * HD)
         own = h * STRETCH
         far = (h + N_HEAD) * STRETCH
         both_ref[own : own + STRETCH, :] = query_ref[rows, part]
-        both_ref[far : far + STRETCH, :] = far_ref[:STRETCH, part]
+        both_ref[far : far + STRETCH, :] = far_ref[:, part]
         own, far = own + COLS, far + COLS
         both_ref[own : own + STRETCH, :] = grad_ref[rows, part]
-        both_ref[far : far + STRETCH, :] = far_ref[STRETCH:, part]
+        both_ref[far : far + STRETCH, :] = far_ref[:, beyond]
     inner = lax.broadcasted_iota(jnp.int32, (8, COLS), 1) % STRETCH
     for side in range(2):
         place = stretches[side] * STRETCH + inner
@@ -200,6 +222,18 @@
     )(*args)
 
 
+def settled(*arrays):
+    wide, thin = shaped(2 * STRETCH, N_HEAD * HD), shaped(2 * STRETCH, HD)
+    return pl.pallas_call(
+        settle,
+        out_shape=(wide, wide, thin, thin),
+        in_specs=[VMEM] * 4,
+        out_specs=(pl.BlockSpec(memory_space=pltpu.HBM),) * 4,
+        scratch_shapes=(pltpu.SemaphoreType.DMA((6,)),),
+        compiler_params=pltpu.CompilerParams(vmem_limit_bytes=2 << 20),
+    )(*arrays)
+
+
 def prepared(docs, query, grad, far):
     outs = (shaped(2 * COLS, HD), shaped(8, 2 * COLS, jnp.int32))
     return run(prepare, outs, (docs, query, grad, far), DOCS * COLS, scalars=1)
@@ -226,20 +260,20 @@
     return run(finish, (half, half, both), (sent, keep), COLS * HD)
 
 
-def paired(array):
-    return lax.all_gather(array, "ctx", axis_index_groups=PAIRS, axis=0, tiled=True)
+def paired(array, axis="ctx", groups=PAIRS):
+    return lax.all_gather(array, axis, axis_index_groups=groups, axis=0, tiled=True)
 
 
 def body(query, key, value, grad_out, doc_lengths):
     lower = lax.axis_index("head") < N_HEAD // 2
     mine = jnp.where(lower, 0, STRETCH)
-    other = STRETCH - mine
-
-    def pick(array, first):
-        return lax.dynamic_slice_in_dim(array, first, STRETCH, 0)
-
-    far = across(jnp.concatenate([pick(query, other), pick(grad_out, other)], axis=0))
-    own = jnp.concatenate([pick(key, mine), pick(value, mine)], axis=1)
+
+    def pick(first, second, start):
+        both = jnp.concatenate([first, second], axis=1)
+        return lax.dynamic_slice_in_dim(both, start, STRETCH, 0)
+
+    own = pick(key, value, mine)
+    far = across(pick(query, grad_out, STRETCH - mine))
     at_4 = along(own, 4 * CHIP)
     two = jnp.concatenate([own, at_4], axis=0)
     at_2_6 = along(two, 2 * CHIP)
@@ -266,23 +300,10 @@
     first = even[: 2 * STRETCH] + home_by(even[2 * STRETCH :], 2)
     back = across(far_out)
     total = (first[:STRETCH] + home_by(first[STRETCH:] + eighth, 4)).astype(jnp.bfloat16)
-    copies = jnp.broadcast_to(total, (N_HEAD,) + total.shape)
-    shared = lax.all_to_all(copies, "head", 0, 0)
-    shared = shared.astype(jnp.float32)
-    kv = jnp.concatenate([shared[0] + shared[1], shared[2] + shared[3]], axis=0)
-    kv = kv.astype(jnp.bfloat16)
-
-    def placed(here, there):
-        return jnp.where(
-            lower, jnp.concatenate([here, there]), jnp.concatenate([there, here])
-        )
-
-    return (
-        placed(out, back[:STRETCH]),
-        placed(dq, back[STRETCH:]),
-        kv[:, :HD],
-        kv[:, HD:],
-    )
+    copies = paired(total, "head", [[0, 1], [2, 3]]).astype(F32)
+    summed = (copies[:STRETCH] + copies[STRETCH:]).astype(jnp.bfloat16)
+    kv = paired(summed, "head", [[0, 3], [1, 2]])
+    return settled(out, dq, back, kv)
 
 
 def solution(mesh):

time: 84.1 us -> 85.9 us (1.021)
  blocking collectives: 6.22 us -> 17.8 us
  starting transfers between devices: 52.3 us -> 44.1 us
  local copies, waits for them, and re-layouts: 3.85 us -> 0.71 us
    all_gather x3 -> x5, blocking collectives: 6.22 us -> 17.8 us  [paired(): lax.all_gather(array, axis, axis_index_groups=groups, axis=0, tiled=True)]
    all_to_all x1 -> x0, starting transfers between devices: 6.32 us -> none  [body(): shared = lax.all_to_all(copies, 'head', 0, 0)]
    ppermute x8, waiting for transfers between devices: 9.73 us -> 15.4 us  [along(): return lax.ppermute(array, BOTH, pairs)]
    all_to_all x1 -> x0, waiting for transfers between devices: 5.22 us -> none  [body(): shared = lax.all_to_all(copies, 'head', 0, 0)]
    dynamic_slice x4 -> x0, local copies, waits for them, and re-layouts: 2.41 us -> none  [pick(): return lax.dynamic_slice_in_dim(array, first, STRETCH, 0)]
    ppermute x8, starting transfers between devices: 34.1 us -> 33.1 us  [along(): return lax.ppermute(array, BOTH, pairs)]
    ppermute x2, starting transfers between devices: 11.9 us -> 11 us  [across(): return lax.ppermute(array, BOTH, pairs)]
  transfers between devices with their start and end apart: 11 -> 10, of which waited for: 6 -> 4; matrix products, arithmetic and copies ran while one was open for 3% -> 1% of each run, Pallas kernels for 2% -> 2%
where the time goes in v1:
time: 85.9 us; the launch traced here: 85.1 us
  starting transfers between devices  44.1 us (51%)
  blocking collectives  17.8 us (21%)
  waiting for transfers between devices  15.4 us (18%)
  Pallas kernels  4.39 us (5%)
  other arithmetic  1.78 us (2%)
  between operations  0.94 us (1%)
    ppermute x8, starting transfers between devices, along(): return lax.ppermute(array, BOTH, pairs)  33.1 us
    all_gather x5, blocking collectives, paired(): lax.all_gather(array, axis, axis_index_groups=groups, axis=0, tiled=True)  17.8 us
    ppermute x8, waiting for transfers between devices, along(): return lax.ppermute(array, BOTH, pairs)  15.4 us
    ppermute x2, starting transfers between devices, across(): return lax.ppermute(array, BOTH, pairs)  11 us
    pallas_call x5, Pallas kernels, run(): pl.pallas_call(kernel, out_shape=outs, in_specs=[SMEM] * scalars + [VMEM]...  3.62 us
  transfers between devices with their start and end apart: 10, of which 4 were waited for; matrix products, arithmetic and copies ran while one was open for 1% of the time, Pallas kernels for 2%

profile of v1, /device:TPU:6, one launch (start us, length us, event | category | flops | bytes accessed | tf_op | source)
XLA Modules:
  0.0 85.1 jit_solution(10042837477134779446)
XLA Ops:
  0.6 0.0 copy-start.1
  0.6 0.0 copy-start
  0.7 0.8 constant_dynamic-update-slice_fusion.4
  1.5 9.1 %collective-permute-start = (bf16[64,256]{1,0:T(8,128)(2,1)S(1)}, bf16[64,256]{1,0:T(8,128)(2,1)S(1)}, u32[]{:S(2)}, u32[]{:S(2)}) collective-permute-start(bf16[64,256]{1,0:T(8,128)(2,1)S(1)} %get-tuple-element.31), channel_id=1, source_target_pairs={{0,32},{1,33},{4,36},{5,37},{8,40},{9,41},{12,44},{13,45},{16,48},... | collective-permute-start | bytes 98312 | tf_op jit(solution)/shard_map/ppermute | solution.py:42
  10.6 0.9 %fusion = bf16[64,1024]{1,0:T(8,128)(2,1)S(1)} fusion(s32[]{:T(128)S(6)} %select_n.9, bf16[128,512]{1,0:T(8,128)(2,1)} %query_ref.1, bf16[128,512]{1,0:T(8,128)(2,1)} %grad_ref.1), kind=kLoop, calls=%fused_computation.3 | loop fusion | flops 262144 | bytes 393220 | tf_op jit(solution)/shard_map/concatenate | solution.py:272
  11.4 8.8 %collective-permute-start.4 = (bf16[64,1024]{1,0:T(8,128)(2,1)S(1)}, bf16[64,1024]{1,0:T(8,128)(2,1)S(1)}, u32[]{:S(2)}, u32[]{:S(2)}) collective-permute-start(bf16[64,1024]{1,0:T(8,128)(2,1)S(1)} %fusion), channel_id=1, source_target_pairs={{0,3},{1,2},{2,1},{3,0},{4,7},{5,6},{6,5},{7,4},{8,11},{9,10},{10,... | collective-permute-start | bytes 393224 | tf_op jit(solution)/shard_map/ppermute | solution.py:49
  20.3 0.0 collective-permute-done
  20.3 3.4 %collective-permute-start.1 = (bf16[128,256]{1,0:T(8,128)(2,1)S(1)}, bf16[128,256]{1,0:T(8,128)(2,1)S(1)}, u32[]{:S(2)}, u32[]{:S(2)}) collective-permute-start(bf16[128,256]{1,0:T(8,128)(2,1)S(1)} %pad_maximum_fusion.1), channel_id=1, source_target_pairs={{0,16},{1,17},{4,20},{5,21},{8,24},{9,25},{12,28},{13,29},{16,32},... | collective-permute-start | bytes 196616 | tf_op jit(solution)/shard_map/ppermute | solution.py:42
  23.7 2.2 %collective-permute-start.3 = (bf16[64,256]{1,0:T(8,128)(2,1)S(1)}, bf16[64,256]{1,0:T(8,128)(2,1)S(1)}, u32[]{:S(2)}, u32[]{:S(2)}) collective-permute-start(bf16[64,256]{1,0:T(8,128)(2,1)S(1)} %collective-permute-done), channel_id=1, source_target_pairs={{0,32},{1,33},{4,36},{5,37},{8,40},{9,41},{12,44},{13,45},{16,48},... | collective-permute-start | bytes 98312 | tf_op jit(solution)/shard_map/ppermute | solution.py:42
  25.9 3.8 %collective-permute-done.1 = bf16[128,256]{1,0:T(8,128)(2,1)S(1)} collective-permute-done((bf16[128,256]{1,0:T(8,128)(2,1)S(1)}, bf16[128,256]{1,0:T(8,128)(2,1)S(1)}, u32[]{:S(2)}, u32[]{:S(2)}) %collective-permute-start.1) | collective-permute-done | bytes 65568 | tf_op jit(solution)/shard_map/ppermute | solution.py:42
  29.7 3.4 %collective-permute-start.2 = (bf16[256,256]{1,0:T(8,128)(2,1)S(1)}, bf16[256,256]{1,0:T(8,128)(2,1)S(1)}, u32[]{:S(2)}, u32[]{:S(2)}) collective-permute-start(bf16[256,256]{1,0:T(8,128)(2,1)S(1)} %pad_maximum_fusion), channel_id=1, source_target_pairs={{0,8},{1,9},{4,12},{5,13},{8,16},{9,17},{12,20},{13,21},{16,24},{1... | collective-permute-start | bytes 393224 | tf_op jit(solution)/shard_map/ppermute | solution.py:42
  33.2 0.0 copy-start.2
  33.2 0.6 copy-done.2
  33.8 0.7 shard_map.84
  34.5 2.2 %all_gather.15.both_ref = bf16[2048,128]{1,0:T(8,128)(2,1)S(1)} all-gather(bf16[1024,128]{1,0:T(8,128)(2,1)S(1)} %get-tuple-element.17), channel_id=1, replica_groups={{0,4},{8,12},{16,20},{24,28},{32,36},{40,44},{48,52},{56,60},{64,68},{7..., dimensions={0}, use_global_device_ids=true | all-gather | bytes 786432 | tf_op jit(solution)/shard_map/all_gather | solution.py:264
  36.7 2.0 %collective-permute-done.2 = bf16[256,256]{1,0:T(8,128)(2,1)S(1)} collective-permute-done((bf16[256,256]{1,0:T(8,128)(2,1)S(1)}, bf16[256,256]{1,0:T(8,128)(2,1)S(1)}, u32[]{:S(2)}, u32[]{:S(2)}) %collective-permute-start.2) | collective-permute-done | bytes 131104 | tf_op jit(solution)/shard_map/ppermute | solution.py:42
  38.7 1.3 %shard_map.85 = (bf16[576,1024]{1,0:T(8,128)(2,1)S(1)}, f32[576,1024]{1,0:T(8,128)S(1)}, f32[8,1024]{1,0:T(8,128)S(1)}) custom-call(bf16[576,256]{1,0:T(8,128)(2,1)S(1)} %constant_dynamic-update-slice_fusion.window_ref, bf16[2048,128]{1,0:T(8,128)(2,1)S(1)} %all_gather.15.both_ref, s32[8,1024]{1,0:T(8,128)S(1)} %get-tuple-element.18.begin_ref), custom_call_target="tpu_custom_call" | custom-call | flops 301989888 | bytes 524288 | tf_op jit(solution)/shard_map/pallas_call | solution.py:214
  40.0 1.9 %all_gather.16.stats_ref = f32[16,1024]{1,0:T(8,128)S(1)} all-gather(f32[8,1024]{1,0:T(8,128)S(1)} %get-tuple-element.21), channel_id=1, replica_groups={{0,4},{8,12},{16,20},{24,28},{32,36},{40,44},{48,52},{56,60},{64,68},{7..., dimensions={0}, use_global_device_ids=true | all-gather | bytes 98304 | tf_op jit(solution)/shard_map/all_gather | solution.py:264
  41.9 1.0 %shard_map.86 = (bf16[576,256]{1,0:T(8,128)(2,1)S(1)}, bf16[576,1024]{1,0:T(8,128)(2,1)S(1)}, bf16[576,1024]{1,0:T(8,128)(2,1)S(1)}) custom-call(bf16[576,256]{1,0:T(8,128)(2,1)S(1)} %constant_dynamic-update-slice_fusion.window_ref, bf16[2048,128]{1,0:T(8,128)(2,1)S(1)} %all_gather.15.both_ref, bf16[576,1024]{1,0:T(8,128)(2,1)S(1)} %get-tuple-element.19.e_ref, ...), custom_call_target="tpu_custom_call" | custom-call | flops 301989888 | bytes 524288 | tf_op jit(solution)/shard_map/pallas_call | solution.py:214
  42.8 2.6 %collective-permute-start.6 = (bf16[256,256]{1,0:T(8,128)(2,1)S(1)}, bf16[256,256]{1,0:T(8,128)(2,1)S(1)}, u32[]{:S(2)}, u32[]{:S(2)}) collective-permute-start(bf16[256,256]{1,0:T(8,128)(2,1)S(1)} %slice.29), channel_id=1, source_target_pairs={{8,0},{9,1},{12,4},{13,5},{16,8},{17,9},{20,12},{21,13},{24,16},{2... | collective-permute-start | bytes 393224 | tf_op jit(solution)/shard_map/ppermute | solution.py:42
  45.4 4.9 %collective-permute-done.6 = bf16[256,256]{1,0:T(8,128)(2,1)S(1)} collective-permute-done((bf16[256,256]{1,0:T(8,128)(2,1)S(1)}, bf16[256,256]{1,0:T(8,128)(2,1)S(1)}, u32[]{:S(2)}, u32[]{:S(2)}) %collective-permute-start.6) | collective-permute-done | bytes 131104 | tf_op jit(solution)/shard_map/ppermute | solution.py:42
  50.3 2.3 %collective-permute-start.7 = (bf16[128,256]{1,0:T(8,128)(2,1)S(1)}, bf16[128,256]{1,0:T(8,128)(2,1)S(1)}, u32[]{:S(2)}, u32[]{:S(2)}) collective-permute-start(bf16[128,256]{1,0:T(8,128)(2,1)S(1)} %slice.56), channel_id=1, source_target_pairs={{16,0},{17,1},{20,4},{21,5},{24,8},{25,9},{28,12},{29,13},{32,16},... | collective-permute-start | bytes 196616 | tf_op jit(solution)/shard_map/ppermute | solution.py:42
  52.7 4.8 %collective-permute-start.8 = (bf16[64,256]{1,0:T(8,128)(2,1)S(1)}, bf16[64,256]{1,0:T(8,128)(2,1)S(1)}, u32[]{:S(2)}, u32[]{:S(2)}) collective-permute-start(bf16[64,256]{1,0:T(8,128)(2,1)S(1)} %slice.34), channel_id=1, source_target_pairs={{32,0},{33,1},{36,4},{37,5},{40,8},{41,9},{44,12},{45,13},{48,16},... | collective-permute-start | bytes 98312 | tf_op jit(solution)/shard_map/ppermute | solution.py:42
  57.5 0.6 shard_map.87
  58.1 4.6 %collective-permute-done.8 = bf16[64,256]{1,0:T(8,128)(2,1)S(1)} collective-permute-done((bf16[64,256]{1,0:T(8,128)(2,1)S(1)}, bf16[64,256]{1,0:T(8,128)(2,1)S(1)}, u32[]{:S(2)}, u32[]{:S(2)}) %collective-permute-start.8) | collective-permute-done | bytes 32800 | tf_op jit(solution)/shard_map/ppermute | solution.py:42
  62.8 5.4 %collective-permute-start.9 = (bf16[64,256]{1,0:T(8,128)(2,1)S(1)}, bf16[64,256]{1,0:T(8,128)(2,1)S(1)}, u32[]{:S(2)}, u32[]{:S(2)}) collective-permute-start(bf16[64,256]{1,0:T(8,128)(2,1)S(1)} %fusion.2), channel_id=1, source_target_pairs={{32,0},{33,1},{36,4},{37,5},{40,8},{41,9},{44,12},{45,13},{48,16},... | collective-permute-start | bytes 98312 | tf_op jit(solution)/shard_map/ppermute | solution.py:42
  68.2 2.2 %all_gather.17.sent_ref = bf16[512,512]{1,0:T(8,128)(2,1)S(1)} all-gather(bf16[256,512]{1,0:T(8,128)(2,1)S(1)} %get-tuple-element.24), channel_id=1, replica_groups={{0,4},{8,12},{16,20},{24,28},{32,36},{40,44},{48,52},{56,60},{64,68},{7..., dimensions={0}, use_global_device_ids=true | all-gather | bytes 786432 | tf_op jit(solution)/shard_map/all_gather | solution.py:264
  70.4 0.1 shard_map.88
  70.5 2.2 %collective-permute-start.5 = (bf16[128,512]{1,0:T(8,128)(2,1)S(1)}, bf16[128,512]{1,0:T(8,128)(2,1)S(1)}, u32[]{:S(2)}, u32[]{:S(2)}) collective-permute-start(bf16[128,512]{1,0:T(8,128)(2,1)S(1)} %get-tuple-element.28), channel_id=1, source_target_pairs={{0,3},{1,2},{2,1},{3,0},{4,7},{5,6},{6,5},{7,4},{8,11},{9,10},{10,... | collective-permute-start | bytes 393224 | tf_op jit(solution)/shard_map/ppermute | solution.py:49
  72.7 4.6 %all_gather.18 = bf16[128,256]{1,0:T(8,128)(2,1)S(1)} all-gather(bf16[64,256]{1,0:T(8,128)(2,1)S(1)} %fusion.3), channel_id=1, replica_groups={{0,1},{2,3},{4,5},{6,7},{8,9},{10,11},{12,13},{14,15},{16,17},{18,19},{..., dimensions={0}, use_global_device_ids=true | all-gather | bytes 98304 | tf_op jit(solution)/shard_map/all_gather | solution.py:264
  77.4 7.0 %all_gather.19.kv_ref = bf16[128,256]{1,0:T(8,128)(2,1)S(1)} all-gather(bf16[64,256]{1,0:T(8,128)(2,1)S(1)} %fusion.1), channel_id=1, replica_groups={{0,3},{1,2},{4,7},{5,6},{8,11},{9,10},{12,15},{13,14},{16,19},{17,18},{..., dimensions={0}, use_global_device_ids=true | all-gather | bytes 98304 | tf_op jit(solution)/shard_map/all_gather | solution.py:264
  84.4 0.8 shard_map.89
  (22 shorter events, 0.2 us)
Async XLA Ops:
  0.6 32.5 %copy-start.1 = (bf16[128,512]{1,0:T(8,128)(2,1)S(1)}, bf16[128,512]{1,0:T(8,128)(2,1)}, u32[]{:S(2)}) copy-start(bf16[128,512]{1,0:T(8,128)(2,1)} %grad_ref.1) | copy-start | bytes 393220
  0.6 32.5 %copy-start = (bf16[128,512]{1,0:T(8,128)(2,1)S(1)}, bf16[128,512]{1,0:T(8,128)(2,1)}, u32[]{:S(2)}) copy-start(bf16[128,512]{1,0:T(8,128)(2,1)} %query_ref.1) | copy-start | bytes 393220
  1.5 18.8 %collective-permute-start = (bf16[64,256]{1,0:T(8,128)(2,1)S(1)}, bf16[64,256]{1,0:T(8,128)(2,1)S(1)}, u32[]{:S(2)}, u32[]{:S(2)}) collective-permute-start(bf16[64,256]{1,0:T(8,128)(2,1)S(1)} %get-tuple-element.31), channel_id=1, source_target_pairs={{0,32},{1,33},{4,36},{5,37},{8,40},{9,41},{12,44},{13,45},{16,48},... | collective-permute-start | bytes 98312 | tf_op jit(solution)/shard_map/ppermute | solution.py:42
  11.4 21.7 %collective-permute-start.4 = (bf16[64,1024]{1,0:T(8,128)(2,1)S(1)}, bf16[64,1024]{1,0:T(8,128)(2,1)S(1)}, u32[]{:S(2)}, u32[]{:S(2)}) collective-permute-start(bf16[64,1024]{1,0:T(8,128)(2,1)S(1)} %fusion), channel_id=1, source_target_pairs={{0,3},{1,2},{2,1},{3,0},{4,7},{5,6},{6,5},{7,4},{8,11},{9,10},{10,... | collective-permute-start | bytes 393224 | tf_op jit(solution)/shard_map/ppermute | solution.py:49
  20.3 9.4 %collective-permute-start.1 = (bf16[128,256]{1,0:T(8,128)(2,1)S(1)}, bf16[128,256]{1,0:T(8,128)(2,1)S(1)}, u32[]{:S(2)}, u32[]{:S(2)}) collective-permute-start(bf16[128,256]{1,0:T(8,128)(2,1)S(1)} %pad_maximum_fusion.1), channel_id=1, source_target_pairs={{0,16},{1,17},{4,20},{5,21},{8,24},{9,25},{12,28},{13,29},{16,32},... | collective-permute-start | bytes 196616 | tf_op jit(solution)/shard_map/ppermute | solution.py:42
  23.7 15.0 %collective-permute-start.3 = (bf16[64,256]{1,0:T(8,128)(2,1)S(1)}, bf16[64,256]{1,0:T(8,128)(2,1)S(1)}, u32[]{:S(2)}, u32[]{:S(2)}) collective-permute-start(bf16[64,256]{1,0:T(8,128)(2,1)S(1)} %collective-permute-done), channel_id=1, source_target_pairs={{0,32},{1,33},{4,36},{5,37},{8,40},{9,41},{12,44},{13,45},{16,48},... | collective-permute-start | bytes 98312 | tf_op jit(solution)/shard_map/ppermute | solution.py:42
  29.7 9.0 %collective-permute-start.2 = (bf16[256,256]{1,0:T(8,128)(2,1)S(1)}, bf16[256,256]{1,0:T(8,128)(2,1)S(1)}, u32[]{:S(2)}, u32[]{:S(2)}) collective-permute-start(bf16[256,256]{1,0:T(8,128)(2,1)S(1)} %pad_maximum_fusion), channel_id=1, source_target_pairs={{0,8},{1,9},{4,12},{5,13},{8,16},{9,17},{12,20},{13,21},{16,24},{1... | collective-permute-start | bytes 393224 | tf_op jit(solution)/shard_map/ppermute | solution.py:42
  33.2 0.7 copy-start.2
  42.8 7.5 %collective-permute-start.6 = (bf16[256,256]{1,0:T(8,128)(2,1)S(1)}, bf16[256,256]{1,0:T(8,128)(2,1)S(1)}, u32[]{:S(2)}, u32[]{:S(2)}) collective-permute-start(bf16[256,256]{1,0:T(8,128)(2,1)S(1)} %slice.29), channel_id=1, source_target_pairs={{8,0},{9,1},{12,4},{13,5},{16,8},{17,9},{20,12},{21,13},{24,16},{2... | collective-permute-start | bytes 393224 | tf_op jit(solution)/shard_map/ppermute | solution.py:42
  50.3 7.8 %collective-permute-start.7 = (bf16[128,256]{1,0:T(8,128)(2,1)S(1)}, bf16[128,256]{1,0:T(8,128)(2,1)S(1)}, u32[]{:S(2)}, u32[]{:S(2)}) collective-permute-start(bf16[128,256]{1,0:T(8,128)(2,1)S(1)} %slice.56), channel_id=1, source_target_pairs={{16,0},{17,1},{20,4},{21,5},{24,8},{25,9},{28,12},{29,13},{32,16},... | collective-permute-start | bytes 196616 | tf_op jit(solution)/shard_map/ppermute | solution.py:42
  52.7 10.1 %collective-permute-start.8 = (bf16[64,256]{1,0:T(8,128)(2,1)S(1)}, bf16[64,256]{1,0:T(8,128)(2,1)S(1)}, u32[]{:S(2)}, u32[]{:S(2)}) collective-permute-start(bf16[64,256]{1,0:T(8,128)(2,1)S(1)} %slice.34), channel_id=1, source_target_pairs={{32,0},{33,1},{36,4},{37,5},{40,8},{41,9},{44,12},{45,13},{48,16},... | collective-permute-start | bytes 98312 | tf_op jit(solution)/shard_map/ppermute | solution.py:42
  62.8 9.9 %collective-permute-start.9 = (bf16[64,256]{1,0:T(8,128)(2,1)S(1)}, bf16[64,256]{1,0:T(8,128)(2,1)S(1)}, u32[]{:S(2)}, u32[]{:S(2)}) collective-permute-start(bf16[64,256]{1,0:T(8,128)(2,1)S(1)} %fusion.2), channel_id=1, source_target_pairs={{32,0},{33,1},{36,4},{37,5},{40,8},{41,9},{44,12},{45,13},{48,16},... | collective-permute-start | bytes 98312 | tf_op jit(solution)/shard_map/ppermute | solution.py:42
  70.5 13.9 %collective-permute-start.5 = (bf16[128,512]{1,0:T(8,128)(2,1)S(1)}, bf16[128,512]{1,0:T(8,128)(2,1)S(1)}, u32[]{:S(2)}, u32[]{:S(2)}) collective-permute-start(bf16[128,512]{1,0:T(8,128)(2,1)S(1)} %get-tuple-element.28), channel_id=1, source_target_pairs={{0,3},{1,2},{2,1},{3,0},{4,7},{5,6},{6,5},{7,4},{8,11},{9,10},{10,... | collective-permute-start | bytes 393224 | tf_op jit(solution)/shard_map/ppermute | solution.py:49

commit v2 on v1

--- a/solution.py
+++ b/solution.py
@@ -78,8 +78,21 @@
         copy.wait()
 
 
-def prepare(docs_ref, query_ref, grad_ref, far_ref, both_ref, begin_ref):
-    _, lower, stretches = place_of()
+def bounds(docs_ref, begin_ref):
+    _, _, stretches = place_of()
+    inner = lax.broadcasted_iota(jnp.int32, (8, COLS), 1) % STRETCH
+    for side in range(2):
+        place = stretches[side] * STRETCH + inner
+        begin = jnp.zeros((8, COLS), jnp.int32)
+        end = jnp.int32(0)
+        for k in range(DOCS):
+            end = end + docs_ref[k]
+            begin = jnp.where(place >= end, end, begin)
+        begin_ref[:, side * COLS : (side + 1) * COLS] = begin
+
+
+def prepare(query_ref, grad_ref, far_ref, both_ref):
+    _, lower, _ = place_of()
     rows = pl.ds(pl.multiple_of(jnp.where(lower, 0, STRETCH), STRETCH), STRETCH)
     for h in range(N_HEAD):
         part = slice(h * HD, (h + 1) * HD)
@@ -91,15 +104,6 @@
         own, far = own + COLS, far + COLS
         both_ref[own : own + STRETCH, :] = grad_ref[rows, part]
         both_ref[far : far + STRETCH, :] = far_ref[:, beyond]
-    inner = lax.broadcasted_iota(jnp.int32, (8, COLS), 1) % STRETCH
-    for side in range(2):
-        place = stretches[side] * STRETCH + inner
-        begin = jnp.zeros((8, COLS), jnp.int32)
-        end = jnp.int32(0)
-        for k in range(DOCS):
-            end = end + docs_ref[k]
-            begin = jnp.where(place >= end, end, begin)
-        begin_ref[:, side * COLS : (side + 1) * COLS] = begin
 
 
 def score(window_ref, both_ref, begin_ref, e_ref, dp_ref, stats_ref, s_sc):
@@ -234,9 +238,12 @@
     )(*arrays)
 
 
-def prepared(docs, query, grad, far):
-    outs = (shaped(2 * COLS, HD), shaped(8, 2 * COLS, jnp.int32))
-    return run(prepare, outs, (docs, query, grad, far), DOCS * COLS, scalars=1)
+def bounded(docs):
+    return run(bounds, (shaped(8, 2 * COLS, jnp.int32),), (docs,), DOCS * COLS, scalars=1)[0]
+
+
+def prepared(query, grad, far):
+    return run(prepare, (shaped(2 * COLS, HD),), (query, grad, far), COLS * HD)[0]
 
 
 def scored(window, both, begin):
@@ -281,7 +288,8 @@
     four = jnp.concatenate([two, at_2_6], axis=0)
     odd = along(four, CHIP)
     parity = jnp.concatenate([four, odd, at_8], axis=0)
-    own_rows, begin = prepared(doc_lengths, query, grad_out, far)
+    begin = bounded(doc_lengths)
+    own_rows = prepared(query, grad_out, far)
     both = paired(own_rows)
     e, dp, stats = scored(parity, both, begin)
     stats = paired(stats)
@@ -300,9 +308,10 @@
     first = even[: 2 * STRETCH] + home_by(even[2 * STRETCH :], 2)
     back = across(far_out)
     total = (first[:STRETCH] + home_by(first[STRETCH:] + eighth, 4)).astype(jnp.bfloat16)
-    copies = paired(total, "head", [[0, 1], [2, 3]]).astype(F32)
-    summed = (copies[:STRETCH] + copies[STRETCH:]).astype(jnp.bfloat16)
-    kv = paired(summed, "head", [[0, 3], [1, 2]])
+    copies = jnp.broadcast_to(total, (N_HEAD,) + total.shape)
+    shared = lax.all_to_all(copies, "head", 0, 0).astype(F32)
+    kv = jnp.concatenate([shared[0] + shared[1], shared[2] + shared[3]], axis=0)
+    kv = kv.astype(jnp.bfloat16)
     return settled(out, dq, back, kv)
 
 

time: 85.9 us -> 91.6 us (1.066)
  blocking collectives: 17.8 us -> 6.2 us
  waiting for transfers between devices: 15.4 us -> 24.7 us
  starting transfers between devices: 44.1 us -> 51.6 us
    all_gather x5 -> x3, blocking collectives: 17.8 us -> 6.2 us  [paired(): lax.all_gather(array, axis, axis_index_groups=groups, axis=0, tiled=True)]
    ppermute x8, waiting for transfers between devices: 15.4 us -> 21 us  [along(): return lax.ppermute(array, BOTH, pairs)]
    all_to_all x0 -> x1, starting transfers between devices: none -> 4.67 us  [body(): shared = lax.all_to_all(copies, 'head', 0, 0).astype(F32)]
    ppermute x2, waiting for transfers between devices: 0.01 us -> 3.71 us  [across(): return lax.ppermute(array, BOTH, pairs)]
    ppermute x2, starting transfers between devices: 11 us -> 14 us  [across(): return lax.ppermute(array, BOTH, pairs)]
    pallas_call x5 -> x6, Pallas kernels: 3.62 us -> 3.64 us  [run(): pl.pallas_call(kernel, out_shape=outs, in_specs=[SMEM] * scalars + [VMEM]...]
  transfers between devices with their start and end apart: 10 -> 11, of which waited for: 4 -> 6; matrix products, arithmetic and copies ran while one was open for 1% -> 1% of each run, Pallas kernels for 2% -> 2%
where the time goes in v2:
time: 91.6 us; the launch traced here: 91 us
  starting transfers between devices  51.6 us (56%)
  waiting for transfers between devices  24.7 us (27%)
  blocking collectives  6.2 us (7%)
  Pallas kernels  4.4 us (5%)
  other arithmetic  1.81 us (2%)
  local copies, waits for them, and re-layouts  1.38 us (2%)
  between operations  0.95 us (1%)
    ppermute x8, starting transfers between devices, along(): return lax.ppermute(array, BOTH, pairs)  33 us
    ppermute x8, waiting for transfers between devices, along(): return lax.ppermute(array, BOTH, pairs)  21 us
    ppermute x2, starting transfers between devices, across(): return lax.ppermute(array, BOTH, pairs)  14 us
    all_gather x3, blocking collectives, paired(): lax.all_gather(array, axis, axis_index_groups=groups, axis=0, tiled=True)  6.2 us
    all_to_all x1, starting transfers between devices, body(): shared = lax.all_to_all(copies, 'head', 0, 0).astype(F32)  4.67 us
    ppermute x2, waiting for transfers between devices, across(): return lax.ppermute(array, BOTH, pairs)  3.71 us
    pallas_call x6, Pallas kernels, run(): pl.pallas_call(kernel, out_shape=outs, in_specs=[SMEM] * scalars + [VMEM]...  3.64 us
  transfers between devices with their start and end apart: 11, of which 6 were waited for; matrix products, arithmetic and copies ran while one was open for 1% of the time, Pallas kernels for 2%

profile of v2, /device:TPU:6, one launch (start us, length us, event | category | flops | bytes accessed | tf_op | source)
XLA Modules:
  0.0 91.0 jit_solution(16628158977024661806)
XLA Ops:
  0.6 0.0 copy-start.1
  0.7 0.8 constant_dynamic-update-slice_fusion.4
  1.5 9.1 %collective-permute-start = (bf16[64,256]{1,0:T(8,128)(2,1)S(1)}, bf16[64,256]{1,0:T(8,128)(2,1)S(1)}, u32[]{:S(2)}, u32[]{:S(2)}) collective-permute-start(bf16[64,256]{1,0:T(8,128)(2,1)S(1)} %get-tuple-element.27), channel_id=1, source_target_pairs={{0,32},{1,33},{4,36},{5,37},{8,40},{9,41},{12,44},{13,45},{16,48},... | collective-permute-start | bytes 98312 | tf_op jit(solution)/shard_map/ppermute | solution.py:42
  10.6 0.9 fusion
  11.4 8.8 %collective-permute-start.4 = (bf16[64,1024]{1,0:T(8,128)(2,1)S(1)}, bf16[64,1024]{1,0:T(8,128)(2,1)S(1)}, u32[]{:S(2)}, u32[]{:S(2)}) collective-permute-start(bf16[64,1024]{1,0:T(8,128)(2,1)S(1)} %fusion), channel_id=1, source_target_pairs={{0,3},{1,2},{2,1},{3,0},{4,7},{5,6},{6,5},{7,4},{8,11},{9,10},{10,... | collective-permute-start | bytes 393224 | tf_op jit(solution)/shard_map/ppermute | solution.py:49
  20.3 0.6 copy-done.2
  20.9 0.6 shard_map.85.begin_ref
  21.6 3.4 %collective-permute-start.1 = (bf16[128,256]{1,0:T(8,128)(2,1)S(1)}, bf16[128,256]{1,0:T(8,128)(2,1)S(1)}, u32[]{:S(2)}, u32[]{:S(2)}) collective-permute-start(bf16[128,256]{1,0:T(8,128)(2,1)S(1)} %pad_maximum_fusion.1), channel_id=1, source_target_pairs={{0,16},{1,17},{4,20},{5,21},{8,24},{9,25},{12,28},{13,29},{16,32},... | collective-permute-start | bytes 196616 | tf_op jit(solution)/shard_map/ppermute | solution.py:42
  25.0 2.2 %collective-permute-start.3 = (bf16[64,256]{1,0:T(8,128)(2,1)S(1)}, bf16[64,256]{1,0:T(8,128)(2,1)S(1)}, u32[]{:S(2)}, u32[]{:S(2)}) collective-permute-start(bf16[64,256]{1,0:T(8,128)(2,1)S(1)} %collective-permute-done), channel_id=1, source_target_pairs={{0,32},{1,33},{4,36},{5,37},{8,40},{9,41},{12,44},{13,45},{16,48},... | collective-permute-start | bytes 98312 | tf_op jit(solution)/shard_map/ppermute | solution.py:42
  27.2 3.8 %collective-permute-done.1 = bf16[128,256]{1,0:T(8,128)(2,1)S(1)} collective-permute-done((bf16[128,256]{1,0:T(8,128)(2,1)S(1)}, bf16[128,256]{1,0:T(8,128)(2,1)S(1)}, u32[]{:S(2)}, u32[]{:S(2)}) %collective-permute-start.1) | collective-permute-done | bytes 65568 | tf_op jit(solution)/shard_map/ppermute | solution.py:42
  31.0 3.4 %collective-permute-start.2 = (bf16[256,256]{1,0:T(8,128)(2,1)S(1)}, bf16[256,256]{1,0:T(8,128)(2,1)S(1)}, u32[]{:S(2)}, u32[]{:S(2)}) collective-permute-start(bf16[256,256]{1,0:T(8,128)(2,1)S(1)} %pad_maximum_fusion), channel_id=1, source_target_pairs={{0,8},{1,9},{4,12},{5,13},{8,16},{9,17},{12,20},{13,21},{16,24},{1... | collective-permute-start | bytes 393224 | tf_op jit(solution)/shard_map/ppermute | solution.py:42
  34.5 0.1 shard_map.84
  34.5 2.2 %all_gather.9.both_ref = bf16[2048,128]{1,0:T(8,128)(2,1)S(1)} all-gather(bf16[1024,128]{1,0:T(8,128)(2,1)S(1)} %shard_map.84), channel_id=1, replica_groups={{0,4},{8,12},{16,20},{24,28},{32,36},{40,44},{48,52},{56,60},{64,68},{7..., dimensions={0}, use_global_device_ids=true | all-gather | bytes 786432 | tf_op jit(solution)/shard_map/all_gather | solution.py:271
  36.7 3.3 %collective-permute-done.2 = bf16[256,256]{1,0:T(8,128)(2,1)S(1)} collective-permute-done((bf16[256,256]{1,0:T(8,128)(2,1)S(1)}, bf16[256,256]{1,0:T(8,128)(2,1)S(1)}, u32[]{:S(2)}, u32[]{:S(2)}) %collective-permute-start.2) | collective-permute-done | bytes 131104 | tf_op jit(solution)/shard_map/ppermute | solution.py:42
  40.0 1.3 %shard_map.86 = (bf16[576,1024]{1,0:T(8,128)(2,1)S(1)}, f32[576,1024]{1,0:T(8,128)S(1)}, f32[8,1024]{1,0:T(8,128)S(1)}) custom-call(bf16[576,256]{1,0:T(8,128)(2,1)S(1)} %constant_dynamic-update-slice_fusion.window_ref, bf16[2048,128]{1,0:T(8,128)(2,1)S(1)} %all_gather.9.both_ref, s32[8,1024]{1,0:T(8,128)S(1)} %shard_map.85.begin_ref), custom_call_target="tpu_custom_call" | custom-call | flops 301989888 | bytes 524288 | tf_op jit(solution)/shard_map/pallas_call | solution.py:218
  41.3 1.9 %all_gather.10.stats_ref = f32[16,1024]{1,0:T(8,128)S(1)} all-gather(f32[8,1024]{1,0:T(8,128)S(1)} %get-tuple-element.17), channel_id=1, replica_groups={{0,4},{8,12},{16,20},{24,28},{32,36},{40,44},{48,52},{56,60},{64,68},{7..., dimensions={0}, use_global_device_ids=true | all-gather | bytes 98304 | tf_op jit(solution)/shard_map/all_gather | solution.py:271
  43.2 1.0 %shard_map.87 = (bf16[576,256]{1,0:T(8,128)(2,1)S(1)}, bf16[576,1024]{1,0:T(8,128)(2,1)S(1)}, bf16[576,1024]{1,0:T(8,128)(2,1)S(1)}) custom-call(bf16[576,256]{1,0:T(8,128)(2,1)S(1)} %constant_dynamic-update-slice_fusion.window_ref, bf16[2048,128]{1,0:T(8,128)(2,1)S(1)} %all_gather.9.both_ref, bf16[576,1024]{1,0:T(8,128)(2,1)S(1)} %get-tuple-element.15.e_ref, ...), custom_call_target="tpu_custom_call" | custom-call | flops 301989888 | bytes 524288 | tf_op jit(solution)/shard_map/pallas_call | solution.py:218
  44.1 1.9 %collective-permute-start.6 = (bf16[256,256]{1,0:T(8,128)(2,1)S(1)}, bf16[256,256]{1,0:T(8,128)(2,1)S(1)}, u32[]{:S(2)}, u32[]{:S(2)}) collective-permute-start(bf16[256,256]{1,0:T(8,128)(2,1)S(1)} %slice.35), channel_id=1, source_target_pairs={{8,0},{9,1},{12,4},{13,5},{16,8},{17,9},{20,12},{21,13},{24,16},{2... | collective-permute-start | bytes 393224 | tf_op jit(solution)/shard_map/ppermute | solution.py:42
  46.1 5.5 %collective-permute-done.6 = bf16[256,256]{1,0:T(8,128)(2,1)S(1)} collective-permute-done((bf16[256,256]{1,0:T(8,128)(2,1)S(1)}, bf16[256,256]{1,0:T(8,128)(2,1)S(1)}, u32[]{:S(2)}, u32[]{:S(2)}) %collective-permute-start.6) | collective-permute-done | bytes 131104 | tf_op jit(solution)/shard_map/ppermute | solution.py:42
  51.7 2.2 %collective-permute-start.7 = (bf16[128,256]{1,0:T(8,128)(2,1)S(1)}, bf16[128,256]{1,0:T(8,128)(2,1)S(1)}, u32[]{:S(2)}, u32[]{:S(2)}) collective-permute-start(bf16[128,256]{1,0:T(8,128)(2,1)S(1)} %slice.78), channel_id=1, source_target_pairs={{16,0},{17,1},{20,4},{21,5},{24,8},{25,9},{28,12},{29,13},{32,16},... | collective-permute-start | bytes 196616 | tf_op jit(solution)/shard_map/ppermute | solution.py:42
  53.9 4.9 %collective-permute-start.8 = (bf16[64,256]{1,0:T(8,128)(2,1)S(1)}, bf16[64,256]{1,0:T(8,128)(2,1)S(1)}, u32[]{:S(2)}, u32[]{:S(2)}) collective-permute-start(bf16[64,256]{1,0:T(8,128)(2,1)S(1)} %slice.40), channel_id=1, source_target_pairs={{32,0},{33,1},{36,4},{37,5},{40,8},{41,9},{44,12},{45,13},{48,16},... | collective-permute-start | bytes 98312 | tf_op jit(solution)/shard_map/ppermute | solution.py:42
  58.8 4.8 %collective-permute-done.8 = bf16[64,256]{1,0:T(8,128)(2,1)S(1)} collective-permute-done((bf16[64,256]{1,0:T(8,128)(2,1)S(1)}, bf16[64,256]{1,0:T(8,128)(2,1)S(1)}, u32[]{:S(2)}, u32[]{:S(2)}) %collective-permute-start.8) | collective-permute-done | bytes 32800 | tf_op jit(solution)/shard_map/ppermute | solution.py:42
  63.6 5.9 %collective-permute-start.9 = (bf16[64,256]{1,0:T(8,128)(2,1)S(1)}, bf16[64,256]{1,0:T(8,128)(2,1)S(1)}, u32[]{:S(2)}, u32[]{:S(2)}) collective-permute-start(bf16[64,256]{1,0:T(8,128)(2,1)S(1)} %fusion.3), channel_id=1, source_target_pairs={{32,0},{33,1},{36,4},{37,5},{40,8},{41,9},{44,12},{45,13},{48,16},... | collective-permute-start | bytes 98312 | tf_op jit(solution)/shard_map/ppermute | solution.py:42
  69.5 0.6 shard_map.88
  70.1 3.6 %collective-permute-done.9 = bf16[64,256]{1,0:T(8,128)(2,1)S(1)} collective-permute-done((bf16[64,256]{1,0:T(8,128)(2,1)S(1)}, bf16[64,256]{1,0:T(8,128)(2,1)S(1)}, u32[]{:S(2)}, u32[]{:S(2)}) %collective-permute-start.9) | collective-permute-done | bytes 32800 | tf_op jit(solution)/shard_map/ppermute | solution.py:42
  73.7 0.7 broadcast_in_dim.3
  74.4 4.7 %all-to-all-start = ((bf16[4,64,256]{2,1,0:T(8,128)(2,1)}), bf16[4,64,256]{2,1,0:T(8,128)(2,1)S(1)}, u32[]{:S(2)}, u32[]{:S(2)}) async-start(bf16[4,64,256]{2,1,0:T(8,128)(2,1)} %broadcast_in_dim.3), calls=%async_computation | async-start | bytes 262144 | tf_op jit(solution)/shard_map/all_to_all | solution.py:312
  79.0 2.2 %all_gather.11.sent_ref = bf16[512,512]{1,0:T(8,128)(2,1)S(1)} all-gather(bf16[256,512]{1,0:T(8,128)(2,1)S(1)} %get-tuple-element.20), channel_id=1, replica_groups={{0,4},{8,12},{16,20},{24,28},{32,36},{40,44},{48,52},{56,60},{64,68},{7..., dimensions={0}, use_global_device_ids=true | all-gather | bytes 786432 | tf_op jit(solution)/shard_map/all_gather | solution.py:271
  81.2 0.1 shard_map.89
  81.4 5.1 %collective-permute-start.5 = (bf16[128,512]{1,0:T(8,128)(2,1)S(1)}, bf16[128,512]{1,0:T(8,128)(2,1)S(1)}, u32[]{:S(2)}, u32[]{:S(2)}) collective-permute-start(bf16[128,512]{1,0:T(8,128)(2,1)S(1)} %get-tuple-element.24), channel_id=1, source_target_pairs={{0,3},{1,2},{2,1},{3,0},{4,7},{5,6},{6,5},{7,4},{8,11},{9,10},{10,... | collective-permute-start | bytes 393224 | tf_op jit(solution)/shard_map/ppermute | solution.py:49
  86.6 3.7 %collective-permute-done.5.back_ref = bf16[128,512]{1,0:T(8,128)(2,1)S(1)} collective-permute-done((bf16[128,512]{1,0:T(8,128)(2,1)S(1)}, bf16[128,512]{1,0:T(8,128)(2,1)S(1)}, u32[]{:S(2)}, u32[]{:S(2)}) %collective-permute-start.5) | collective-permute-done | bytes 131104 | tf_op jit(solution)/shard_map/ppermute | solution.py:49
  90.3 0.8 shard_map.90
  (25 shorter events, 0.2 us)
Async XLA Ops:
  0.6 33.8 %copy-start.1 = (bf16[128,512]{1,0:T(8,128)(2,1)S(1)}, bf16[128,512]{1,0:T(8,128)(2,1)}, u32[]{:S(2)}) copy-start(bf16[128,512]{1,0:T(8,128)(2,1)} %grad_ref.1) | copy-start | bytes 393220
  0.6 33.8 %copy-start = (bf16[128,512]{1,0:T(8,128)(2,1)S(1)}, bf16[128,512]{1,0:T(8,128)(2,1)}, u32[]{:S(2)}) copy-start(bf16[128,512]{1,0:T(8,128)(2,1)} %query_ref.1) | copy-start | bytes 393220
  1.5 20.1 %collective-permute-start = (bf16[64,256]{1,0:T(8,128)(2,1)S(1)}, bf16[64,256]{1,0:T(8,128)(2,1)S(1)}, u32[]{:S(2)}, u32[]{:S(2)}) collective-permute-start(bf16[64,256]{1,0:T(8,128)(2,1)S(1)} %get-tuple-element.27), channel_id=1, source_target_pairs={{0,32},{1,33},{4,36},{5,37},{8,40},{9,41},{12,44},{13,45},{16,48},... | collective-permute-start | bytes 98312 | tf_op jit(solution)/shard_map/ppermute | solution.py:42
  11.4 23.0 %collective-permute-start.4 = (bf16[64,1024]{1,0:T(8,128)(2,1)S(1)}, bf16[64,1024]{1,0:T(8,128)(2,1)S(1)}, u32[]{:S(2)}, u32[]{:S(2)}) collective-permute-start(bf16[64,1024]{1,0:T(8,128)(2,1)S(1)} %fusion), channel_id=1, source_target_pairs={{0,3},{1,2},{2,1},{3,0},{4,7},{5,6},{6,5},{7,4},{8,11},{9,10},{10,... | collective-permute-start | bytes 393224 | tf_op jit(solution)/shard_map/ppermute | solution.py:49
  20.3 0.7 copy-start.2
  21.6 9.4 %collective-permute-start.1 = (bf16[128,256]{1,0:T(8,128)(2,1)S(1)}, bf16[128,256]{1,0:T(8,128)(2,1)S(1)}, u32[]{:S(2)}, u32[]{:S(2)}) collective-permute-start(bf16[128,256]{1,0:T(8,128)(2,1)S(1)} %pad_maximum_fusion.1), channel_id=1, source_target_pairs={{0,16},{1,17},{4,20},{5,21},{8,24},{9,25},{12,28},{13,29},{16,32},... | collective-permute-start | bytes 196616 | tf_op jit(solution)/shard_map/ppermute | solution.py:42
  25.0 15.0 %collective-permute-start.3 = (bf16[64,256]{1,0:T(8,128)(2,1)S(1)}, bf16[64,256]{1,0:T(8,128)(2,1)S(1)}, u32[]{:S(2)}, u32[]{:S(2)}) collective-permute-start(bf16[64,256]{1,0:T(8,128)(2,1)S(1)} %collective-permute-done), channel_id=1, source_target_pairs={{0,32},{1,33},{4,36},{5,37},{8,40},{9,41},{12,44},{13,45},{16,48},... | collective-permute-start | bytes 98312 | tf_op jit(solution)/shard_map/ppermute | solution.py:42
  31.0 9.0 %collective-permute-start.2 = (bf16[256,256]{1,0:T(8,128)(2,1)S(1)}, bf16[256,256]{1,0:T(8,128)(2,1)S(1)}, u32[]{:S(2)}, u32[]{:S(2)}) collective-permute-start(bf16[256,256]{1,0:T(8,128)(2,1)S(1)} %pad_maximum_fusion), channel_id=1, source_target_pairs={{0,8},{1,9},{4,12},{5,13},{8,16},{9,17},{12,20},{13,21},{16,24},{1... | collective-permute-start | bytes 393224 | tf_op jit(solution)/shard_map/ppermute | solution.py:42
  44.1 7.5 %collective-permute-start.6 = (bf16[256,256]{1,0:T(8,128)(2,1)S(1)}, bf16[256,256]{1,0:T(8,128)(2,1)S(1)}, u32[]{:S(2)}, u32[]{:S(2)}) collective-permute-start(bf16[256,256]{1,0:T(8,128)(2,1)S(1)} %slice.35), channel_id=1, source_target_pairs={{8,0},{9,1},{12,4},{13,5},{16,8},{17,9},{20,12},{21,13},{24,16},{2... | collective-permute-start | bytes 393224 | tf_op jit(solution)/shard_map/ppermute | solution.py:42
  51.7 7.1 %collective-permute-start.7 = (bf16[128,256]{1,0:T(8,128)(2,1)S(1)}, bf16[128,256]{1,0:T(8,128)(2,1)S(1)}, u32[]{:S(2)}, u32[]{:S(2)}) collective-permute-start(bf16[128,256]{1,0:T(8,128)(2,1)S(1)} %slice.78), channel_id=1, source_target_pairs={{16,0},{17,1},{20,4},{21,5},{24,8},{25,9},{28,12},{29,13},{32,16},... | collective-permute-start | bytes 196616 | tf_op jit(solution)/shard_map/ppermute | solution.py:42
  53.9 9.7 %collective-permute-start.8 = (bf16[64,256]{1,0:T(8,128)(2,1)S(1)}, bf16[64,256]{1,0:T(8,128)(2,1)S(1)}, u32[]{:S(2)}, u32[]{:S(2)}) collective-permute-start(bf16[64,256]{1,0:T(8,128)(2,1)S(1)} %slice.40), channel_id=1, source_target_pairs={{32,0},{33,1},{36,4},{37,5},{40,8},{41,9},{44,12},{45,13},{48,16},... | collective-permute-start | bytes 98312 | tf_op jit(solution)/shard_map/ppermute | solution.py:42
  63.6 10.1 %collective-permute-start.9 = (bf16[64,256]{1,0:T(8,128)(2,1)S(1)}, bf16[64,256]{1,0:T(8,128)(2,1)S(1)}, u32[]{:S(2)}, u32[]{:S(2)}) collective-permute-start(bf16[64,256]{1,0:T(8,128)(2,1)S(1)} %fusion.3), channel_id=1, source_target_pairs={{32,0},{33,1},{36,4},{37,5},{40,8},{41,9},{44,12},{45,13},{48,16},... | collective-permute-start | bytes 98312 | tf_op jit(solution)/shard_map/ppermute | solution.py:42
  74.4 12.1 %all-to-all-start = ((bf16[4,64,256]{2,1,0:T(8,128)(2,1)}), bf16[4,64,256]{2,1,0:T(8,128)(2,1)S(1)}, u32[]{:S(2)}, u32[]{:S(2)}) async-start(bf16[4,64,256]{2,1,0:T(8,128)(2,1)} %broadcast_in_dim.3), calls=%async_computation | async-start | bytes 262144 | tf_op jit(solution)/shard_map/all_to_all | solution.py:312
  81.4 8.9 %collective-permute-start.5 = (bf16[128,512]{1,0:T(8,128)(2,1)S(1)}, bf16[128,512]{1,0:T(8,128)(2,1)S(1)}, u32[]{:S(2)}, u32[]{:S(2)}) collective-permute-start(bf16[128,512]{1,0:T(8,128)(2,1)S(1)} %get-tuple-element.24), channel_id=1, source_target_pairs={{0,3},{1,2},{2,1},{3,0},{4,7},{5,6},{6,5},{7,4},{8,11},{9,10},{10,... | collective-permute-start | bytes 393224 | tf_op jit(solution)/shard_map/ppermute | solution.py:49
